TPU v7x, 256 devices: a whole 4x4x8 slice. The times are simulated.
256 devices in a mesh: grp: 8 (over z_hi, core), dev: 32 (over z_lo, y, x).
Axes of the slice: x: 4, y: 4, z: 8 (z_hi: 4, z_lo: 2; z = z_hi * 2 + z_lo), core: 2. Of those that a mesh axis runs over, the one named last changes fastest.
Arguments:
- user_factors: float32 [32768, 256], P(('grp', 'dev')), may hold values from -0.5 to 0.5
- item_factors: float32 [16384, 256], P(('grp', 'dev')), may hold values from -0.5 to 0.5
- user_items: int32 [32768, 8, 3], P(('grp', 'dev')), may hold values from 0 to 2047, as said below
- user_conf: float32 [32768, 8, 3], P(('grp', 'dev')), may hold values from 1 to 200
- user_mask: int32 [32768, 8, 3], P(('grp', 'dev')), may hold values 0 or 1
- item_users: int32 [16384, 8, 6], P(('grp', 'dev')), may hold values from 0 to 4095, as said below
- item_conf: float32 [16384, 8, 6], P(('grp', 'dev')), may hold values from 1 to 200
- item_mask: int32 [16384, 8, 6], P(('grp', 'dev')), may hold values 0 or 1
Outputs:
- new_users: float32 [32768, 256], P(('grp', 'dev'))
- new_items: float32 [16384, 256], P(('grp', 'dev'))
Inputs may be any that keep to these rules, and one draw needn't show every extreme that they name: Within owner block c, id // 64 is the owner device and id % 64 its row. The user_items of the users of one device, in one owner block, name at most 16 distinct rows of any one owner device, and in every block each device names exactly 16 distinct rows of some owner device. Within owner block c, id // 128 is the owner device and id % 128 its row. The item_users of the items of one device, in one owner block, name at most 16 distinct rows of any one owner device, and in every block each device names exactly 16 distinct rows of some owner device.
All inputs are finite; a program needn't handle non-finite values. No bound on the sum of `user_mask` or of `item_mask` on one device may be relied on, other than what follows from the above.
Results may differ from a plain program's by a relative error of at most 0.0044.
Values may be sent and summed in bfloat16 or wider, within the bound.
A program may use at most 128 MiB of HBM per device.

v0:
```python
import jax
import jax.numpy as jnp
from jax import lax
from jax.sharding import Mesh
from jax.sharding import PartitionSpec as P

CG_STEPS = 4
GRP = ("grp_0", "grp_1")
GRP_DEV = ("grp_0", "grp_1", "dev")
ridge = 1.0


def joined_along(blocks, dim):
    dims = list(blocks.shape[1:])
    dims[dim] *= blocks.shape[0]
    return jnp.moveaxis(blocks, 0, dim).reshape(dims)


def gather_in_order(array, axes, turns):
    blocks = array
    for k in turns:
        blocks = lax.all_gather(blocks, axes[k])
    done = turns[::-1]
    back = [done.index(k) for k in range(len(axes))]
    blocks = blocks.transpose(*back, *range(len(axes), blocks.ndim))
    return blocks.reshape(-1, *array.shape)


def whole_of(array, axes, turns, dim):
    return joined_along(gather_in_order(array, axes, turns), dim)


def solve_rows(gram, start_x, rows, confidence, slot_mask):
    maskf = slot_mask.astype(jnp.float32)
    weight = confidence * maskf
    rhs = jnp.einsum(
        "us,usr->ur", maskf * (1.0 + confidence), rows, precision=lax.Precision.HIGHEST
    )

    def apply(vector):
        along = jnp.einsum("usr,ur->us", rows, vector, precision=lax.Precision.HIGHEST)
        extra = jnp.einsum("us,usr->ur", weight * along, rows, precision=lax.Precision.HIGHEST)
        return jnp.dot(vector, gram, precision=lax.Precision.HIGHEST) + ridge * vector + extra

    solution = start_x
    resid = rhs - apply(solution)
    direction = resid
    norm_now = jnp.sum(resid * resid, axis=1, keepdims=True)
    for step in range(CG_STEPS):
        image = apply(direction)
        alpha = norm_now / jnp.sum(direction * image, axis=1, keepdims=True)
        solution = solution + alpha * direction
        resid = resid - alpha * image
        norm_next = jnp.sum(resid * resid, axis=1, keepdims=True)
        direction = resid + norm_next / norm_now * direction
        norm_now = norm_next
    return solution


def gram_of(block):
    return lax.dot_general(
        block, block, (((0,), (0,)), ((), ())), preferred_element_type=jnp.float32
    )


def collect(whole, row_index, mask_now):
    picked = jnp.take(whole, row_index, axis=0).astype(jnp.float32)
    return picked * mask_now[..., None].astype(jnp.float32)


def half_step(start_x, other, slot_ids, confidence, slot_mask):
    local_rows = other.shape[0]
    groups = lax.axis_size(GRP)
    packed = other.astype(jnp.bfloat16)
    row_parts = []
    conf_parts = []
    mask_parts = []
    stacked = whole_of(packed, GRP, (0, 1), 0)
    whole = lax.all_gather(stacked, "dev", axis=0, tiled=True)
    for span in range(groups):
        local = slot_ids[:, span, :]
        row_index = (
            local // local_rows * (groups * local_rows) + span * local_rows + local % local_rows
        )
        row_parts.append(collect(whole, row_index, slot_mask[:, span, :]))
        conf_parts.append(confidence[:, span, :])
        mask_parts.append(slot_mask[:, span, :])
    squares = gram_of(whole)
    rows = jnp.concatenate(row_parts, axis=1)
    conf_all = jnp.concatenate(conf_parts, axis=1)
    mask_all = jnp.concatenate(mask_parts, axis=1)
    return solve_rows(squares, start_x, rows, conf_all, mask_all)


def per_device(
    user_factors, item_factors, user_items, user_conf, user_mask, item_users, item_conf, item_mask
):
    new_users = half_step(user_factors, item_factors, user_items, user_conf, user_mask)
    new_items = half_step(item_factors, new_users, item_users, item_conf, item_mask)
    return (new_users, new_items)


def solution(mesh):
    finer = Mesh(mesh.devices.reshape(4, 2, mesh.shape["dev"]), ("grp_0", "grp_1", "dev"))
    in_specs = (
        P(GRP_DEV, None),
        P(GRP_DEV, None),
        P(GRP_DEV, None, None),
        P(GRP_DEV, None, None),
        P(GRP_DEV, None, None),
        P(GRP_DEV, None, None),
        P(GRP_DEV, None, None),
        P(GRP_DEV, None, None),
    )
    out_specs = (P(GRP_DEV, None), P(GRP_DEV, None))
    return jax.shard_map(
        per_device, mesh=finer, in_specs=in_specs, out_specs=out_specs, check_vma=False
    )
```

profile of v0, /device:TPU:1, one launch (start us, length us, event | category | flops | bytes accessed | tf_op | source)
XLA Modules:
  0.0 744.5 jit_solution(14757438769674752799)
XLA Ops:
  8.1 15.5 %all-gather = bf16[256,256]{1,0:T(8,128)(2,1)S(1)} all-gather(bf16[64,256]{1,0:T(8,128)(2,1)S(1)} %convert_element_type.189), channel_id=2, replica_groups=mesh['grp_0'=4,'grp_1'=2,'dev'=32] {'grp_0'}, dimensions={0}, use_global_device_ids=true | all-gather | bytes 163840 | tf_op jit(solution)/shard_map/all_gather | solution.py:22
  23.6 5.0 all-gather.1
  38.0 139.0 %all-gather.7.cloned.1.call-done = bf16[16384,256]{1,0:T(8,128)(2,1)} async-done(((bf16[512,256]{1,0:T(8,128)(2,1)}), bf16[16384,256]{1,0:T(8,128)(2,1)}) %all-gather.7.cloned.1.call-update) | async-done | bytes 8388624 | tf_op jit(solution)/shard_map/all_gather | solution.py:79
  177.0 6.1 gather_fusion.7
  183.2 6.1 gather_fusion.6
  189.5 6.1 gather_fusion.5
  195.7 6.1 gather_fusion.4
  202.0 6.1 gather_fusion.3
  208.2 6.7 gather_fusion.2
  215.0 6.1 gather_fusion.1
  221.2 6.1 gather_fusion
  236.6 22.3 %concatenate.20 = f32[128,24,256]{2,1,0:T(8,128)S(1)} concatenate(f32[128,3,256]{2,1,0:T(4,128)} %convert_multiply_fusion.15, f32[128,3,256]{2,1,0:T(4,128)} %convert_multiply_fusion.14, f32[128,3,256]{2,1,0:T(4,128)} %convert_multiply_fusion.13, f32[128,3,256]{2,1,0:T(4,128)} %convert_multiply_fusion.12, f32[128,3,256]{2,1,0:T(4,128)} %convert_multiply_fusion.11, ...), dimensions={1} | concatenate | bytes 6291456 | tf_op jit(solution)/shard_map/concatenate | solution.py:89
  258.9 2.8 fusion.18
  264.8 8.2 %fusion.190 = f32[256,256]{1,0:T(8,128)S(1)} fusion(bf16[16384,256]{1,0:T(8,128)(2,1)} %all-gather.7.cloned.1.call-done), kind=kOutput, calls=%fused_computation.457 | convolution fusion | flops 2147483648 | bytes 8650752 | tf_op jit(solution)/shard_map/dot_general | solution.py:61
  337.5 13.1 %all-gather.2 = bf16[512,256]{0,1:T(8,128)(2,1)S(1)} all-gather(bf16[128,256]{0,1:T(8,128)(2,1)S(1)} %get-tuple-element.36), channel_id=4, replica_groups=mesh['grp_0'=4,'grp_1'=2,'dev'=32] {'grp_0'}, dimensions={0}, use_global_device_ids=true | all-gather | bytes 327680 | tf_op jit(solution)/shard_map/all_gather | solution.py:22
  350.7 25.6 %all-gather.3 = bf16[8,128,256]{2,1,0:T(8,128)(2,1)S(1)} all-gather(bf16[4,128,256]{2,1,0:T(8,128)(2,1)S(1)} %bitcast.642), channel_id=5, replica_groups=mesh['grp_0'=4,'grp_1'=2,'dev'=32] {'grp_1'}, dimensions={0}, use_global_device_ids=true | all-gather | bytes 786432 | tf_op jit(solution)/shard_map/all_gather | solution.py:22
  383.0 185.0 %all-gather.9.cloned.1.call-done = bf16[32768,256]{1,0:T(8,128)(2,1)} async-done(((bf16[1024,256]{1,0:T(8,128)(2,1)}), bf16[32768,256]{1,0:T(8,128)(2,1)}) %all-gather.9.cloned.1.call-update) | async-done | bytes 16777232 | tf_op jit(solution)/shard_map/all_gather | solution.py:79
  568.0 9.6 %gather_fusion.15 = bf16[384,256]{1,0:T(8,128)(2,1)S(1)} fusion(bf16[32768,256]{1,0:T(8,128)(2,1)} %all-gather.9.cloned.1.call-done, s32[1024]{0:T(1024)S(1)} %pad_clamp_fusion), kind=kCustom, calls=%fused_computation.15.clone | custom fusion | bytes 394752 | tf_op jit(solution)/shard_map/jit(_take)/gather | solution.py:67
  577.7 9.6 %gather_fusion.14 = bf16[384,256]{1,0:T(8,128)(2,1)S(1)} fusion(bf16[32768,256]{1,0:T(8,128)(2,1)} %all-gather.9.cloned.1.call-done, s32[1024]{0:T(1024)S(1)} %pad_clamp_fusion.1), kind=kCustom, calls=%fused_computation.14.clone | custom fusion | bytes 394752 | tf_op jit(solution)/shard_map/jit(_take)/gather | solution.py:67
  587.4 9.6 %gather_fusion.13 = bf16[384,256]{1,0:T(8,128)(2,1)S(1)} fusion(bf16[32768,256]{1,0:T(8,128)(2,1)} %all-gather.9.cloned.1.call-done, s32[1024]{0:T(1024)S(1)} %pad_clamp_fusion.2), kind=kCustom, calls=%fused_computation.13.clone | custom fusion | bytes 394752 | tf_op jit(solution)/shard_map/jit(_take)/gather | solution.py:67
  597.0 9.8 %gather_fusion.12 = bf16[384,256]{1,0:T(8,128)(2,1)S(1)} fusion(bf16[32768,256]{1,0:T(8,128)(2,1)} %all-gather.9.cloned.1.call-done, s32[1024]{0:T(1024)S(1)} %pad_clamp_fusion.3), kind=kCustom, calls=%fused_computation.12.clone | custom fusion | bytes 394752 | tf_op jit(solution)/shard_map/jit(_take)/gather | solution.py:67
  606.9 9.6 %gather_fusion.11 = bf16[384,256]{1,0:T(8,128)(2,1)S(1)} fusion(bf16[32768,256]{1,0:T(8,128)(2,1)} %all-gather.9.cloned.1.call-done, s32[1024]{0:T(1024)S(1)} %pad_clamp_fusion.4), kind=kCustom, calls=%fused_computation.11.clone | custom fusion | bytes 394752 | tf_op jit(solution)/shard_map/jit(_take)/gather | solution.py:67
  616.6 9.6 %gather_fusion.10 = bf16[384,256]{1,0:T(8,128)(2,1)S(1)} fusion(bf16[32768,256]{1,0:T(8,128)(2,1)} %all-gather.9.cloned.1.call-done, s32[1024]{0:T(1024)S(1)} %pad_clamp_fusion.5), kind=kCustom, calls=%fused_computation.10.clone | custom fusion | bytes 394752 | tf_op jit(solution)/shard_map/jit(_take)/gather | solution.py:67
  626.3 9.6 %gather_fusion.9 = bf16[384,256]{1,0:T(8,128)(2,1)S(1)} fusion(bf16[32768,256]{1,0:T(8,128)(2,1)} %all-gather.9.cloned.1.call-done, s32[1024]{0:T(1024)S(1)} %pad_clamp_fusion.6), kind=kCustom, calls=%fused_computation.9.clone | custom fusion | bytes 394752 | tf_op jit(solution)/shard_map/jit(_take)/gather | solution.py:67
  635.9 9.8 %gather_fusion.8 = bf16[384,256]{1,0:T(8,128)(2,1)S(1)} fusion(bf16[32768,256]{1,0:T(8,128)(2,1)} %all-gather.9.cloned.1.call-done, s32[1024]{0:T(1024)S(1)} %pad_clamp_fusion.7), kind=kCustom, calls=%fused_computation.1.clone | custom fusion | bytes 394752 | tf_op jit(solution)/shard_map/jit(_take)/gather | solution.py:67
  653.8 20.6 %concatenate.23 = f32[64,48,256]{2,1,0:T(8,128)S(1)} concatenate(f32[64,6,256]{2,1,0:T(8,128)} %convert_multiply_fusion.7, f32[64,6,256]{2,1,0:T(8,128)} %convert_multiply_fusion.6, f32[64,6,256]{2,1,0:T(8,128)} %convert_multiply_fusion.5, f32[64,6,256]{2,1,0:T(8,128)} %convert_multiply_fusion.4, f32[64,6,256]{2,1,0:T(8,128)} %convert_multiply_fusion.3, ...), dimensions={1} | concatenate | bytes 6291456 | tf_op jit(solution)/shard_map/concatenate | solution.py:89
  674.4 2.8 fusion.28
  682.0 14.5 %fusion.192 = f32[256,256]{1,0:T(8,128)S(1)} fusion(bf16[32768,256]{1,0:T(8,128)(2,1)} %all-gather.9.cloned.1.call-done), kind=kOutput, calls=%fused_computation.459 | convolution fusion | flops 4294967296 | bytes 17039360 | tf_op jit(solution)/shard_map/dot_general | solution.py:61
  696.8 2.8 fusion.26
  702.4 3.4 fusion.24
  714.3 3.4 fusion.22
  726.3 3.4 fusion.20
  (313 shorter events, 135.3 us)
Async XLA Ops:
  7.2 29.2 %copy-start.5 = (f32[128,256]{1,0:T(8,128)S(1)}, f32[128,256]{1,0:T(8,128)}, u32[]{:S(2)}) copy-start(f32[128,256]{1,0:T(8,128)} %param.12) | copy-start | bytes 393220
  7.2 29.9 %copy-start.23 = (f32[128,8,3]{0,1,2:T(8,128)S(1)}, f32[128,8,3]{0,1,2:T(8,128)}, u32[]{:S(2)}) copy-start(f32[128,8,3]{0,1,2:T(8,128)} %param.15) | copy-start | bytes 36868
  7.2 169.8 %all-gather.7.cloned.1.call-start = ((), (), s32[]{:S(2)}) async-start(), calls=%async_computation | async-start | bytes 8650752 | tf_op jit(solution)/shard_map/all_gather | solution.py:79
  29.4 538.6 %all-gather.9.cloned.1.call-start = ((), (), s32[]{:S(2)}) async-start(), calls=%async_computation.1 | async-start | bytes 17301504 | tf_op jit(solution)/shard_map/all_gather | solution.py:79
  264.8 8.2 %copy-start.6 = (f32[128,256]{1,0:T(8,128)S(1)}, f32[128,256]{1,0:T(8,128)}, u32[]{:S(2)}) copy-start(f32[128,256]{1,0:T(8,128)} %param.12) | copy-start | bytes 393220
  264.8 8.2 %copy-start.7 = (f32[128,256]{0,1:T(8,128)S(1)}, f32[128,256]{0,1:T(8,128)}, u32[]{:S(2)}) copy-start(f32[128,256]{0,1:T(8,128)} %copy.246) | copy-start | bytes 393220
  264.8 8.2 %copy-start.17 = (f32[128,256]{0,1:T(8,128)S(1)}, f32[128,256]{0,1:T(8,128)}, u32[]{:S(2)}) copy-start(f32[128,256]{0,1:T(8,128)} %copy.310) | copy-start | bytes 393220
  264.8 8.2 %copy-start.18 = (f32[128,256]{0,1:T(8,128)S(1)}, f32[128,256]{0,1:T(8,128)}, u32[]{:S(2)}) copy-start(f32[128,256]{0,1:T(8,128)} %copy.304) | copy-start | bytes 393220
  286.0 0.7 copy-start
  286.1 0.6 copy-start.26
  301.4 1.0 copy-start.25
  302.4 0.5 copy-start.27
  302.4 1.2 copy-start.1
  319.2 2.1 copy-start.24
  333.1 44.0 %copy-start.20 = (s32[64,8,6]{0,1,2:T(8,128)S(1)}, s32[64,8,6]{0,1,2:T(8,128)}, u32[]{:S(2)}) copy-start(s32[64,8,6]{0,1,2:T(8,128)} %param.17) | copy-start | bytes 36868
  333.1 45.1 %copy-start.21 = (s32[64,8,6]{0,1,2:T(8,128)S(1)}, s32[64,8,6]{0,1,2:T(8,128)}, u32[]{:S(2)}) copy-start(s32[64,8,6]{0,1,2:T(8,128)} %param.19) | copy-start | bytes 36868
  333.1 47.8 %copy-start.22 = (f32[64,8,6]{0,1,2:T(8,128)S(1)}, f32[64,8,6]{0,1,2:T(8,128)}, u32[]{:S(2)}) copy-start(f32[64,8,6]{0,1,2:T(8,128)} %param.18) | copy-start | bytes 36868
  653.8 20.6 %copy-start.14 = (f32[64,256]{1,0:T(8,128)S(1)}, f32[64,256]{1,0:T(8,128)}, u32[]{:S(2)}) copy-start(f32[64,256]{1,0:T(8,128)} %param.13) | copy-start | bytes 196612
  682.0 14.5 %copy-start.19 = (f32[64,1,256]{2,1,0:T(1,128)S(1)}, f32[64,1,256]{2,1,0:T(1,128)}, u32[]{:S(2)}) copy-start(f32[64,1,256]{2,1,0:T(1,128)} %fusion.193) | copy-start | bytes 196612
  696.8 2.8 copy-start.16
  701.7 0.6 copy-start.8
  710.0 2.8 copy-start.9
  713.0 0.6 copy-start.10
  713.7 0.6 copy-start.2
  722.0 2.6 copy-start.3
  722.0 3.0 copy-start.11
  725.1 0.6 copy-start.29
  725.7 0.6 copy-start.12
  726.3 10.4 %copy-start.30 = (f32[64]{0:T(128)S(1)}, f32[64]{0:T(128)}, u32[]{:S(2)}) copy-start(f32[64]{0:T(128)} %copy-done.29) | copy-start | bytes 772
  733.9 2.4 copy-start.13
  733.9 2.8 copy-start.4
  733.9 2.8 copy-start.15
  (1 other events, 0.5 us)
Sparse Core Ops, SparseCore 0:
  29.5 147.4 all-gather.6
  377.2 190.7 all-gather.8
where the time goes:
time: 751 us; the launch traced here: 745 us
  waiting for transfers between devices  324 us (43%)
  local copies, waits for them, and re-layouts  225 us (30%)
  matrix products  62.8 us (8%)
  blocking collectives  59.2 us (8%)
  other arithmetic  58.1 us (8%)
  between operations  15.2 us (2%)
    all_gather x2, waiting for transfers between devices, half_step(): whole = lax.all_gather(stacked, 'dev', axis=0, tiled=True)  324 us
    gather x32, local copies, waits for them, and re-layouts, collect(): picked = jnp.take(whole, row_index, axis=0).astype(jnp.float32)  128 us
    all_gather x4, blocking collectives, gather_in_order(): blocks = lax.all_gather(blocks, axes[k])  59.2 us
    concatenate x2, local copies, waits for them, and re-layouts, half_step(): rows = jnp.concatenate(row_parts, axis=1)  42.9 us
    dot_general x2, matrix products, gram_of(): lax.dot_general(block, block, (((0,), (0,)), ((), ())), preferred_element...  22.7 us
    dot_general x6, matrix products, apply(): jnp.einsum('usr,ur->us', rows, vector, precision=lax.Precision.HIGHEST)  18.5 us
    unnamed x9, other arithmetic  18 us
    unnamed x74, local copies, waits for them, and re-layouts  17.6 us
  transfers between devices with their start and end apart: 2, of which 2 were waited for; matrix products, arithmetic and copies ran while one was open for 2% of the time, Pallas kernels for 0%

commit v1 on v0

--- a/solution.py
+++ b/solution.py
@@ -76,7 +76,9 @@
     conf_parts = []
     mask_parts = []
     stacked = whole_of(packed, GRP, (0, 1), 0)
-    whole = lax.all_gather(stacked, "dev", axis=0, tiled=True)
+    whole = jnp.concatenate(
+        lax.all_to_all(jnp.stack([stacked] * lax.axis_size("dev")), "dev", 0, 0), axis=0
+    )
     for span in range(groups):
         local = slot_ids[:, span, :]
         row_index = (

time: 751 us -> 827 us (1.10)
  the two profiles are of different devices: /device:TPU:1 before, /device:TPU:52 now
where the time goes in v1:
time: 827 us; the launch traced here: 814 us
  waiting for transfers between devices  405 us (49%)
  local copies, waits for them, and re-layouts  231 us (28%)
  matrix products  62.7 us (8%)
  other arithmetic  58.1 us (7%)
  blocking collectives  37.6 us (5%)
  starting transfers between devices  17.4 us (2%)
    all_to_all x2, waiting for transfers between devices, half_step(): lax.all_to_all(jnp.stack([stacked] * lax.axis_size('dev')), 'dev', 0, 0)  405 us
    gather x32, local copies, waits for them, and re-layouts, collect(): picked = jnp.take(whole, row_index, axis=0).astype(jnp.float32)  128 us
    concatenate x2, local copies, waits for them, and re-layouts, half_step(): rows = jnp.concatenate(row_parts, axis=1)  42.9 us
    all_gather x4, blocking collectives, gather_in_order(): blocks = lax.all_gather(blocks, axes[k])  37.6 us
    dot_general x2, matrix products, gram_of(): lax.dot_general(block, block, (((0,), (0,)), ((), ())), preferred_element...  22.5 us
    dot_general x6, matrix products, apply(): jnp.einsum('usr,ur->us', rows, vector, precision=lax.Precision.HIGHEST)  18.5 us
    unnamed x9, other arithmetic  18 us
    unnamed x78, local copies, waits for them, and re-layouts  17.6 us
  transfers between devices with their start and end apart: 2, of which 2 were waited for; matrix products, arithmetic and copies ran while one was open for 1% of the time, Pallas kernels for 0%

profile of v1, /device:TPU:52, one launch (start us, length us, event | category | flops | bytes accessed | tf_op | source)
XLA Modules:
  0.0 813.7 jit_solution(12083694416337913886)
XLA Ops:
  1.5 16.5 %all-gather = bf16[256,256]{1,0:T(8,128)(2,1)S(1)} all-gather(bf16[64,256]{1,0:T(8,128)(2,1)S(1)} %convert_element_type.189), channel_id=2, replica_groups=mesh['grp_0'=4,'grp_1'=2,'dev'=32] {'grp_0'}, dimensions={0}, use_global_device_ids=true | all-gather | bytes 163840 | tf_op jit(solution)/shard_map/all_gather | solution.py:22
  20.0 4.2 stack.6
  24.2 8.5 %all-to-all-start = ((bf16[32,512,256]{2,1,0:T(8,128)(2,1)}), bf16[32,512,256]{2,1,0:T(8,128)(2,1)}, u32[]{:S(2)}, u32[]{:S(2)}) async-start(bf16[32,512,256]{2,1,0:T(8,128)(2,1)} %stack.6), calls=%async_computation | async-start | bytes 16777216 | tf_op jit(solution)/shard_map/all_to_all | solution.py:80
  38.8 125.1 %all-to-all-done = bf16[32,512,256]{2,1,0:T(8,128)(2,1)} async-done(((bf16[32,512,256]{2,1,0:T(8,128)(2,1)}), bf16[32,512,256]{2,1,0:T(8,128)(2,1)}, u32[]{:S(2)}, u32[]{:S(2)}) %all-to-all-start) | async-done | bytes 8388640 | tf_op jit(solution)/shard_map/all_to_all | solution.py:80
  164.0 6.1 gather_fusion
  170.2 6.1 gather_fusion.1
  176.5 6.1 gather_fusion.2
  182.7 6.1 gather_fusion.3
  188.9 6.5 gather_fusion.4
  195.5 6.1 gather_fusion.5
  201.8 6.1 gather_fusion.6
  208.0 6.1 gather_fusion.7
  223.4 22.3 %concatenate.20 = f32[128,24,256]{2,1,0:T(8,128)S(1)} concatenate(f32[128,3,256]{2,1,0:T(4,128)} %convert_multiply_fusion.15, f32[128,3,256]{2,1,0:T(4,128)} %convert_multiply_fusion.14, f32[128,3,256]{2,1,0:T(4,128)} %convert_multiply_fusion.13, f32[128,3,256]{2,1,0:T(4,128)} %convert_multiply_fusion.12, f32[128,3,256]{2,1,0:T(4,128)} %convert_multiply_fusion.11, ...), dimensions={1} | concatenate | bytes 6291456 | tf_op jit(solution)/shard_map/concatenate | solution.py:91
  245.7 2.8 fusion.18
  251.6 8.2 %convolution_bitcast_fusion.1 = f32[256,256]{1,0:T(8,128)S(1)} fusion(bf16[32,512,256]{2,1,0:T(8,128)(2,1)} %all-to-all-done), kind=kOutput, calls=%fused_computation.27 | convolution fusion | flops 2147483648 | bytes 8650752 | tf_op jit(solution)/shard_map/dot_general | solution.py:61
  324.2 16.9 %all-gather.2 = bf16[512,256]{0,1:T(8,128)(2,1)S(1)} all-gather(bf16[128,256]{0,1:T(8,128)(2,1)S(1)} %get-tuple-element.36), channel_id=4, replica_groups=mesh['grp_0'=4,'grp_1'=2,'dev'=32] {'grp_0'}, dimensions={0}, use_global_device_ids=true | all-gather | bytes 327680 | tf_op jit(solution)/shard_map/all_gather | solution.py:22
  343.5 5.9 stack.7
  349.4 8.9 %all-to-all-start.1 = ((bf16[32,1024,256]{2,1,0:T(8,128)(2,1)}), bf16[32,1024,256]{2,1,0:T(8,128)(2,1)}, u32[]{:S(2)}, u32[]{:S(2)}) async-start(bf16[32,1024,256]{2,1,0:T(8,128)(2,1)} %stack.7), calls=%async_computation.1 | async-start | bytes 33554432 | tf_op jit(solution)/shard_map/all_to_all | solution.py:80
  363.9 279.8 %all-to-all-done.1 = bf16[32,1024,256]{2,1,0:T(8,128)(2,1)} async-done(((bf16[32,1024,256]{2,1,0:T(8,128)(2,1)}), bf16[32,1024,256]{2,1,0:T(8,128)(2,1)}, u32[]{:S(2)}, u32[]{:S(2)}) %all-to-all-start.1) | async-done | bytes 16777248 | tf_op jit(solution)/shard_map/all_to_all | solution.py:80
  643.7 9.6 %gather_fusion.8 = bf16[384,256]{1,0:T(8,128)(2,1)S(1)} fusion(bf16[32768,256]{1,0:T(8,128)(2,1)} %bitcast.57, s32[1024]{0:T(1024)S(1)} %pad_clamp_fusion.7), kind=kCustom, calls=%fused_computation.1.clone | custom fusion | bytes 394752 | tf_op jit(solution)/shard_map/jit(_take)/gather | solution.py:67
  653.3 9.6 %gather_fusion.9 = bf16[384,256]{1,0:T(8,128)(2,1)S(1)} fusion(bf16[32768,256]{1,0:T(8,128)(2,1)} %bitcast.57, s32[1024]{0:T(1024)S(1)} %pad_clamp_fusion.6), kind=kCustom, calls=%fused_computation.9.clone | custom fusion | bytes 394752 | tf_op jit(solution)/shard_map/jit(_take)/gather | solution.py:67
  663.0 10.0 %gather_fusion.10 = bf16[384,256]{1,0:T(8,128)(2,1)S(1)} fusion(bf16[32768,256]{1,0:T(8,128)(2,1)} %bitcast.57, s32[1024]{0:T(1024)S(1)} %pad_clamp_fusion.5), kind=kCustom, calls=%fused_computation.10.clone | custom fusion | bytes 394752 | tf_op jit(solution)/shard_map/jit(_take)/gather | solution.py:67
  673.1 9.6 %gather_fusion.11 = bf16[384,256]{1,0:T(8,128)(2,1)S(1)} fusion(bf16[32768,256]{1,0:T(8,128)(2,1)} %bitcast.57, s32[1024]{0:T(1024)S(1)} %pad_clamp_fusion.4), kind=kCustom, calls=%fused_computation.11.clone | custom fusion | bytes 394752 | tf_op jit(solution)/shard_map/jit(_take)/gather | solution.py:67
  682.8 9.6 %gather_fusion.12 = bf16[384,256]{1,0:T(8,128)(2,1)S(1)} fusion(bf16[32768,256]{1,0:T(8,128)(2,1)} %bitcast.57, s32[1024]{0:T(1024)S(1)} %pad_clamp_fusion.3), kind=kCustom, calls=%fused_computation.12.clone | custom fusion | bytes 394752 | tf_op jit(solution)/shard_map/jit(_take)/gather | solution.py:67
  692.5 9.6 %gather_fusion.13 = bf16[384,256]{1,0:T(8,128)(2,1)S(1)} fusion(bf16[32768,256]{1,0:T(8,128)(2,1)} %bitcast.57, s32[1024]{0:T(1024)S(1)} %pad_clamp_fusion.2), kind=kCustom, calls=%fused_computation.13.clone | custom fusion | bytes 394752 | tf_op jit(solution)/shard_map/jit(_take)/gather | solution.py:67
  702.2 9.8 %gather_fusion.14 = bf16[384,256]{1,0:T(8,128)(2,1)S(1)} fusion(bf16[32768,256]{1,0:T(8,128)(2,1)} %bitcast.57, s32[1024]{0:T(1024)S(1)} %pad_clamp_fusion.1), kind=kCustom, calls=%fused_computation.14.clone | custom fusion | bytes 394752 | tf_op jit(solution)/shard_map/jit(_take)/gather | solution.py:67
  712.0 9.6 %gather_fusion.15 = bf16[384,256]{1,0:T(8,128)(2,1)S(1)} fusion(bf16[32768,256]{1,0:T(8,128)(2,1)} %bitcast.57, s32[1024]{0:T(1024)S(1)} %pad_clamp_fusion), kind=kCustom, calls=%fused_computation.15.clone | custom fusion | bytes 394752 | tf_op jit(solution)/shard_map/jit(_take)/gather | solution.py:67
  729.7 20.6 %concatenate.23 = f32[64,48,256]{2,1,0:T(8,128)S(1)} concatenate(f32[64,6,256]{2,1,0:T(8,128)} %convert_multiply_fusion.7, f32[64,6,256]{2,1,0:T(8,128)} %convert_multiply_fusion.6, f32[64,6,256]{2,1,0:T(8,128)} %convert_multiply_fusion.5, f32[64,6,256]{2,1,0:T(8,128)} %convert_multiply_fusion.4, f32[64,6,256]{2,1,0:T(8,128)} %convert_multiply_fusion.3, ...), dimensions={1} | concatenate | bytes 6291456 | tf_op jit(solution)/shard_map/concatenate | solution.py:91
  757.8 14.3 %convolution_bitcast_fusion = f32[256,256]{1,0:T(8,128)S(1)} fusion(bf16[32,1024,256]{2,1,0:T(8,128)(2,1)} %all-to-all-done.1), kind=kOutput, calls=%fused_computation.26 | convolution fusion | flops 4294967296 | bytes 17039360 | tf_op jit(solution)/shard_map/dot_general | solution.py:61
  778.1 3.4 fusion.24
  790.0 3.4 fusion.22
  802.1 3.4 fusion.20
  (317 shorter events, 140.6 us)
Async XLA Ops:
  24.1 8.5 %copy-start.23 = (s32[128,8,3]{0,1,2:T(8,128)S(1)}, s32[128,8,3]{0,1,2:T(8,128)}, u32[]{:S(2)}) copy-start(s32[128,8,3]{0,1,2:T(8,128)} %param.14) | copy-start | bytes 36868
  24.1 8.9 %copy-start.24 = (s32[128,8,3]{0,1,2:T(8,128)S(1)}, s32[128,8,3]{0,1,2:T(8,128)}, u32[]{:S(2)}) copy-start(s32[128,8,3]{0,1,2:T(8,128)} %param.16) | copy-start | bytes 36868
  24.1 13.3 %copy-start.5 = (f32[128,256]{1,0:T(8,128)S(1)}, f32[128,256]{1,0:T(8,128)}, u32[]{:S(2)}) copy-start(f32[128,256]{1,0:T(8,128)} %param.12) | copy-start | bytes 393220
  24.1 14.1 %copy-start.25 = (f32[128,8,3]{0,1,2:T(8,128)S(1)}, f32[128,8,3]{0,1,2:T(8,128)}, u32[]{:S(2)}) copy-start(f32[128,8,3]{0,1,2:T(8,128)} %param.15) | copy-start | bytes 36868
  24.2 139.8 %all-to-all-start = ((bf16[32,512,256]{2,1,0:T(8,128)(2,1)}), bf16[32,512,256]{2,1,0:T(8,128)(2,1)}, u32[]{:S(2)}, u32[]{:S(2)}) async-start(bf16[32,512,256]{2,1,0:T(8,128)(2,1)} %stack.6), calls=%async_computation | async-start | bytes 16777216 | tf_op jit(solution)/shard_map/all_to_all | solution.py:80
  251.6 8.2 %copy-start.6 = (f32[128,256]{1,0:T(8,128)S(1)}, f32[128,256]{1,0:T(8,128)}, u32[]{:S(2)}) copy-start(f32[128,256]{1,0:T(8,128)} %param.12) | copy-start | bytes 393220
  251.6 8.2 %copy-start.7 = (f32[128,256]{0,1:T(8,128)S(1)}, f32[128,256]{0,1:T(8,128)}, u32[]{:S(2)}) copy-start(f32[128,256]{0,1:T(8,128)} %copy.252) | copy-start | bytes 393220
  251.6 8.2 %copy-start.17 = (f32[128,256]{0,1:T(8,128)S(1)}, f32[128,256]{0,1:T(8,128)}, u32[]{:S(2)}) copy-start(f32[128,256]{0,1:T(8,128)} %copy.311) | copy-start | bytes 393220
  251.6 8.2 %copy-start.18 = (f32[128,256]{0,1:T(8,128)S(1)}, f32[128,256]{0,1:T(8,128)}, u32[]{:S(2)}) copy-start(f32[128,256]{0,1:T(8,128)} %copy.318) | copy-start | bytes 393220
  272.8 0.7 copy-start
  272.8 0.6 copy-start.28
  288.2 1.0 copy-start.27
  289.2 1.2 copy-start.1
  306.0 2.1 copy-start.26
  349.4 8.9 %copy-start.20 = (s32[64,8,6]{0,1,2:T(8,128)S(1)}, s32[64,8,6]{0,1,2:T(8,128)}, u32[]{:S(2)}) copy-start(s32[64,8,6]{0,1,2:T(8,128)} %param.17) | copy-start | bytes 36868
  349.4 9.2 %copy-start.21 = (s32[64,8,6]{0,1,2:T(8,128)S(1)}, s32[64,8,6]{0,1,2:T(8,128)}, u32[]{:S(2)}) copy-start(s32[64,8,6]{0,1,2:T(8,128)} %param.19) | copy-start | bytes 36868
  349.4 12.7 %copy-start.22 = (f32[64,8,6]{0,1,2:T(8,128)S(1)}, f32[64,8,6]{0,1,2:T(8,128)}, u32[]{:S(2)}) copy-start(f32[64,8,6]{0,1,2:T(8,128)} %param.18) | copy-start | bytes 36868
  349.4 294.2 %all-to-all-start.1 = ((bf16[32,1024,256]{2,1,0:T(8,128)(2,1)}), bf16[32,1024,256]{2,1,0:T(8,128)(2,1)}, u32[]{:S(2)}, u32[]{:S(2)}) async-start(bf16[32,1024,256]{2,1,0:T(8,128)(2,1)} %stack.7), calls=%async_computation.1 | async-start | bytes 33554432 | tf_op jit(solution)/shard_map/all_to_all | solution.py:80
  729.7 20.6 %copy-start.14 = (f32[64,256]{1,0:T(8,128)S(1)}, f32[64,256]{1,0:T(8,128)}, u32[]{:S(2)}) copy-start(f32[64,256]{1,0:T(8,128)} %param.13) | copy-start | bytes 196612
  757.8 14.3 %copy-start.19 = (f32[64,1,256]{2,1,0:T(1,128)S(1)}, f32[64,1,256]{2,1,0:T(1,128)}, u32[]{:S(2)}) copy-start(f32[64,1,256]{2,1,0:T(1,128)} %fusion.191) | copy-start | bytes 196612
  772.4 2.8 copy-start.16
  777.4 0.6 copy-start.8
  785.7 2.8 copy-start.9
  788.7 0.6 copy-start.10
  789.4 0.6 copy-start.2
  797.6 2.7 copy-start.3
  797.6 3.0 copy-start.11
  801.4 0.6 copy-start.12
  802.1 10.4 %copy-start.32 = (f32[64]{0:T(128)S(1)}, f32[64]{0:T(128)}, u32[]{:S(2)}) copy-start(f32[64]{0:T(128)} %copy-done.31) | copy-start | bytes 772
  809.7 2.4 copy-start.13
  809.7 2.8 copy-start.4
  809.7 2.8 copy-start.15
  (3 other events, 1.6 us)
